TPU v7x, 128 devices: a whole 4x4x4 slice. The times are simulated.
128 devices in a mesh: dp: 16 (over x_lo, y, core), tensor: 8 (over x_hi, z).
Axes of the slice: x: 4 (x_hi: 2, x_lo: 2; x = x_hi * 2 + x_lo), y: 4, z: 4, core: 2. Of those that a mesh axis runs over, the one named last changes fastest.
Arguments:
- block_input: bfloat16 [32768, 768], P(('dp', 'tensor')), may hold values from -6 to 6
- w_value: bfloat16 [768, 768], replicated, may hold values from -0.21875 to 0.21875
- b_value: bfloat16 [768], replicated, may hold values from -2 to 2
- conv_kernel: bfloat16 [65, 768], replicated, may hold values from -0.75 to 0.75
- w_out: bfloat16 [768, 768], replicated, may hold values from -0.21875 to 0.21875
- b_out: bfloat16 [768], replicated, may hold values from -2 to 2
- gain_attn: bfloat16 [768], replicated, may hold values from 0.5 to 1.5
- shift_attn: bfloat16 [768], replicated, may hold values from -2 to 2
- w_up: bfloat16 [768, 3072], P(None, 'tensor'), may hold values from -0.21875 to 0.21875
- b_up: bfloat16 [3072], P('tensor'), may hold values from -2 to 2
- w_down: bfloat16 [3072, 768], P('tensor'), may hold values from -0.109375 to 0.109375
- b_down: bfloat16 [768], replicated, may hold values from -2 to 2
- gain_ffn: bfloat16 [768], replicated, may hold values from 0.5 to 1.5
- shift_ffn: bfloat16 [768], replicated, may hold values from -2 to 2
- query_codes: int32 [32768, 384], P(('dp', 'tensor')), may hold values from 0 to 255
- key_codes: int32 [32768, 384], P(('dp', 'tensor')), may hold values from 0 to 255
- key_live: int32 [32768], P(('dp', 'tensor')), may hold values 0 or 1
- seq_lengths: int32 [128, 4], P(('dp', 'tensor')), may hold values from 1 to 128, 256 in all within a row
- out_grad: bfloat16 [32768, 768], P(('dp', 'tensor')), may hold values from -6 to 6
Outputs:
- block_output: bfloat16 [32768, 768], P(('dp', 'tensor'))
- input_grad: float32 [32768, 768], P(('dp', 'tensor'))
- grad_w_value: float32 [768, 768], replicated
- grad_b_value: float32 [768], replicated
- grad_conv_kernel: float32 [65, 768], replicated
- grad_w_out: float32 [768, 768], replicated
- grad_b_out: float32 [768], replicated
- grad_gain_attn: float32 [768], replicated
- grad_shift_attn: float32 [768], replicated
- grad_w_up: float32 [768, 3072], P(None, 'tensor')
- grad_b_up: float32 [3072], P('tensor')
- grad_w_down: float32 [3072, 768], P('tensor')
- grad_b_down: float32 [768], replicated
- grad_gain_ffn: float32 [768], replicated
- grad_shift_ffn: float32 [768], replicated
Inputs may be any that keep to these rules, and one draw needn't show every extreme that they name: `seq_lengths`: each item's lengths sum to 256; the longest is 128. `key_live`: 1 marks a live key, 0 a padded one. `query_codes`: column h * 32 + s holds head h's code in hash set s. `key_codes`: column h * 32 + s holds head h's code in hash set s.
All inputs are finite; a program needn't handle non-finite values. No bound on the sum of `key_live` on one device may be relied on, other than what follows from the above.
Results may differ from a plain program's by a relative error of at most 0.02.
Values may be sent and summed in bfloat16 or wider, within the bound.
No kernel may reach another device: no remote copies, remote signals or barrier semaphores. Data moves between devices by JAX's collectives and lax.ppermute only.
A program may use at most 128 MiB of HBM per device.

v0:
```python
from functools import partial
import jax
import jax.numpy as jnp
from jax import lax
from jax.sharding import PartitionSpec as P

HEADS = 12
SETS = 32
BUCKETS = 256


def dot_last(former, latter):
    return lax.dot_general(
        former, latter, (((1,), (1,)), ((), ())), preferred_element_type=jnp.float32
    )


def dot_first(former, latter):
    return lax.dot_general(
        former, latter, (((0,), (0,)), ((), ())), preferred_element_type=jnp.float32
    )


def layer_norm(residual, gain_vec, shift_vec):
    average = jnp.mean(residual, axis=-1, keepdims=True)
    centred = residual - average
    variance = jnp.mean(centred * centred, axis=-1, keepdims=True)
    return centred * lax.rsqrt(variance + 1e-05) * gain_vec + shift_vec


def head_norm(mixed, head_count, head_dim):
    grouped = mixed.reshape(mixed.shape[0], head_count, head_dim)
    scaling = lax.rsqrt(jnp.mean(grouped * grouped, axis=-1, keepdims=True) + 1e-06)
    return (grouped * scaling).reshape(mixed.shape)


def gelu_exact(pre_act):
    return jax.nn.gelu(pre_act, approximate=False)


def depth_conv(values, kernel, segment):
    taps = kernel.shape[0]
    margin = taps // 2
    length = values.shape[0]
    padded = jnp.pad(values, ((margin, margin), (0, 0)))
    seg_padded = jnp.pad(segment, (margin, margin), constant_values=-1)
    running = jnp.zeros_like(values)
    for offset in range(taps):
        joined = (seg_padded[offset : offset + length] == segment).astype(jnp.float32)[:, None]
        running = running + padded[offset : offset + length] * joined * kernel[offset][None, :]
    return running


def conv_back(grad_out, values, kernel, segment):
    taps = kernel.shape[0]
    margin = taps // 2
    length = values.shape[0]
    padded = jnp.pad(values, ((margin, margin), (0, 0)))
    grad_padded = jnp.pad(grad_out, ((margin, margin), (0, 0)))
    seg_padded = jnp.pad(segment, (margin, margin), constant_values=-1)
    value_grad = jnp.zeros_like(values)
    tap_rows = []
    for offset in range(taps):
        joined = (seg_padded[offset : offset + length] == segment).astype(jnp.float32)[:, None]
        tap_rows.append(jnp.sum(grad_out * joined * padded[offset : offset + length], axis=0))
        mirror = 2 * margin - offset
        back_joined = (seg_padded[mirror : mirror + length] == segment).astype(jnp.float32)[:, None]
        value_grad = (
            value_grad
            + grad_padded[mirror : mirror + length] * back_joined * kernel[offset][None, :]
        )
    return (value_grad, jnp.stack(tap_rows, axis=0))


def body(
    block_input,
    w_value,
    b_value,
    conv_kernel,
    w_out,
    b_out,
    gain_attn,
    shift_attn,
    w_up,
    b_up,
    w_down,
    b_down,
    gain_ffn,
    shift_ffn,
    query_codes,
    key_codes,
    key_live,
    seq_lengths,
    out_grad,
):
    length = block_input.shape[0]
    model_width = block_input.shape[1]
    head_dim = model_width // HEADS
    live_keys = key_live.astype(jnp.float32)[:, None]
    seq_ends = jnp.cumsum(seq_lengths[0], dtype=jnp.int32)
    positions = jnp.arange(length, dtype=jnp.int32)
    segment = jnp.sum(
        (seq_ends[None, :] <= positions[:, None]).astype(jnp.int32), axis=1, dtype=jnp.int32
    )
    query_heads = query_codes.reshape(length, HEADS, SETS).transpose(1, 0, 2)
    key_heads = key_codes.reshape(length, HEADS, SETS).transpose(1, 0, 2)
    joined = (segment[:, None] == segment[None, :]).astype(jnp.float32)
    bucket_ids = jnp.arange(BUCKETS, dtype=jnp.int32)

    def head_counts(pair):
        query_set, key_set = pair
        query_hot = (
            (query_set[:, :, None] == bucket_ids[None, None, :])
            .astype(jnp.bfloat16)
            .reshape(length, SETS * BUCKETS)
        )
        key_hot = (
            (key_set[:, :, None] == bucket_ids[None, None, :])
            .astype(jnp.bfloat16)
            .reshape(length, SETS * BUCKETS)
        )
        counts = dot_last(query_hot, key_hot)
        return (counts * joined / SETS).astype(jnp.bfloat16)

    collide = lax.map(head_counts, (query_heads, key_heads))
    kernel_f = conv_kernel.astype(jnp.float32)
    value_pre = jnp.dot(block_input, w_value, preferred_element_type=jnp.float32) + b_value.astype(
        jnp.float32
    )
    values = value_pre.astype(jnp.bfloat16)
    masked = values.astype(jnp.float32) * live_keys
    masked_low = masked.astype(jnp.bfloat16)
    mixed = jnp.einsum(
        "hij,jhd->ihd",
        collide,
        masked_low.reshape(length, HEADS, head_dim),
        preferred_element_type=jnp.float32,
    ).reshape(length, model_width)
    normed, norm_back = jax.vjp(partial(head_norm, head_count=HEADS, head_dim=head_dim), mixed)
    context = (normed + depth_conv(masked, kernel_f, segment)).astype(jnp.bfloat16)
    attended = jnp.dot(context, w_out, preferred_element_type=jnp.float32) + b_out.astype(
        jnp.float32
    )
    first, first_back = jax.vjp(
        layer_norm,
        block_input.astype(jnp.float32) + attended,
        gain_attn.astype(jnp.float32),
        shift_attn.astype(jnp.float32),
    )
    first_low = first.astype(jnp.bfloat16)
    gathered = lax.all_gather(first_low, "tensor", axis=0, tiled=True)
    upper = jnp.dot(gathered, w_up, preferred_element_type=jnp.float32) + b_up.astype(jnp.float32)
    active_f, gelu_back = jax.vjp(gelu_exact, upper)
    active = active_f.astype(jnp.bfloat16)
    branch = lax.psum_scatter(
        jnp.dot(active, w_down, preferred_element_type=jnp.float32).astype(jnp.bfloat16),
        "tensor",
        scatter_dimension=0,
        tiled=True,
    ).astype(jnp.float32) + b_down.astype(jnp.float32)
    block_output, second_back = jax.vjp(
        layer_norm, first + branch, gain_ffn.astype(jnp.float32), shift_ffn.astype(jnp.float32)
    )
    grad_second, grad_gain_ffn, grad_shift_ffn = second_back(out_grad.astype(jnp.float32))
    branch_grad = grad_second.astype(jnp.bfloat16)
    grad_b_down = jnp.sum(branch_grad.astype(jnp.float32), axis=0)
    grad_rows_all = lax.all_gather(branch_grad, "tensor", axis=0, tiled=True)
    active_grad = dot_last(grad_rows_all, w_down)
    grad_w_down = dot_first(active, grad_rows_all)
    upper_grad = gelu_back(active_grad)[0].astype(jnp.bfloat16)
    grad_w_up = dot_first(gathered, upper_grad)
    grad_b_up = jnp.sum(upper_grad.astype(jnp.float32), axis=0)
    first_grad_ffn = lax.psum_scatter(
        dot_last(upper_grad, w_up).astype(jnp.bfloat16), "tensor", scatter_dimension=0, tiled=True
    ).astype(jnp.float32)
    first_grad = grad_second + first_grad_ffn
    resid_grad, grad_gain_attn, grad_shift_attn = first_back(first_grad)
    attended_grad = resid_grad.astype(jnp.bfloat16)
    grad_b_out = jnp.sum(attended_grad.astype(jnp.float32), axis=0)
    grad_w_out = dot_first(context, attended_grad)
    context_grad = dot_last(attended_grad, w_out)
    mixed_grad = norm_back(context_grad)[0].astype(jnp.bfloat16)
    conv_value_grad, grad_kernel = conv_back(context_grad, masked, kernel_f, segment)
    masked_att = jnp.einsum(
        "hij,ihd->jhd",
        collide,
        mixed_grad.reshape(length, HEADS, head_dim),
        preferred_element_type=jnp.float32,
    ).reshape(length, model_width)
    value_grad = ((masked_att + conv_value_grad) * live_keys).astype(jnp.bfloat16)
    grad_b_value = jnp.sum(value_grad.astype(jnp.float32), axis=0)
    grad_w_value = dot_first(block_input, value_grad)
    input_grad = resid_grad + dot_last(value_grad, w_value)
    grad_w_up, grad_w_down, grad_b_up = (
        lax.psum(grad_w_up.astype(jnp.bfloat16), "dp").astype(jnp.float32),
        lax.psum(grad_w_down.astype(jnp.bfloat16), "dp").astype(jnp.float32),
        lax.psum(grad_b_up.astype(jnp.bfloat16), "dp").astype(jnp.float32),
    )
    (
        grad_w_value,
        grad_b_value,
        grad_kernel,
        grad_w_out,
        grad_b_out,
        grad_gain_attn,
        grad_shift_attn,
        grad_b_down,
        grad_gain_ffn,
        grad_shift_ffn,
    ) = lax.psum(
        (
            grad_w_value,
            grad_b_value,
            grad_kernel,
            grad_w_out,
            grad_b_out,
            grad_gain_attn,
            grad_shift_attn,
            grad_b_down,
            grad_gain_ffn,
            grad_shift_ffn,
        ),
        ("dp", "tensor"),
    )
    return (
        block_output.astype(jnp.bfloat16),
        input_grad,
        grad_w_value,
        grad_b_value,
        grad_kernel,
        grad_w_out,
        grad_b_out,
        grad_gain_attn,
        grad_shift_attn,
        grad_w_up,
        grad_b_up,
        grad_w_down,
        grad_b_down,
        grad_gain_ffn,
        grad_shift_ffn,
    )


def solution(mesh):
    return jax.shard_map(
        body,
        mesh=mesh,
        in_specs=(
            P(("dp", "tensor"), None),
            P(),
            P(),
            P(),
            P(),
            P(),
            P(),
            P(),
            P(None, "tensor"),
            P("tensor"),
            P("tensor", None),
            P(),
            P(),
            P(),
            P(("dp", "tensor"), None),
            P(("dp", "tensor"), None),
            P(("dp", "tensor")),
            P(("dp", "tensor"), None),
            P(("dp", "tensor"), None),
        ),
        out_specs=(
            P(("dp", "tensor"), None),
            P(("dp", "tensor"), None),
            P(),
            P(),
            P(),
            P(),
            P(),
            P(),
            P(),
            P(None, "tensor"),
            P("tensor"),
            P("tensor", None),
            P(),
            P(),
            P(),
        ),
        check_vma=False,
    )
```

profile of v0, /device:TPU:1, one launch (start us, length us, event | category | flops | bytes accessed | tf_op | source)
XLA Modules:
  0.0 701.4 jit_solution(10940862884612107198)
XLA Ops:
  15.0 1.2 copy.49
  16.1 1.2 copy.50
  17.3 43.1 %while.12 = (s32[]{:T(128)}, bf16[12,256,256]{2,1,0:T(8,128)(2,1)}, s32[12,256,32]{1,2,0:T(8,128)S(1)}, s32[12,256,32]{1,2,0:T(8,128)S(1)}, s32[256]{0:T(256)S(1)}, /*index=5*/s32[]{:T(128)}) while((s32[]{:T(128)}, bf16[12,256,256]{2,1,0:T(8,128)(2,1)}, s32[12,256,32]{1,2,0:T(8,128)S(1)}, s32[12,256,32]{1,2,0:T(8,128)S(1)}, ...), condition=%wide.region_3.4_spmd.clone.clone, body=%wide.region_2.3_spmd.clone.clone.sunk | while | flops 1078198272 | bytes 330313 | solution.py:125
  17.4 3.6 fusion.266
  21.0 3.6 fusion.266
  24.6 3.6 fusion.266
  28.1 3.6 fusion.266
  31.7 3.6 fusion.266
  35.3 3.6 fusion.266
  38.9 3.6 fusion.266
  42.5 3.6 fusion.266
  46.1 3.6 fusion.266
  49.7 3.6 fusion.266
  53.3 3.6 fusion.266
  56.8 3.6 fusion.266
  61.2 2.0 multiply_reduce_fusion.70
  64.2 1.4 copy.51
  66.3 11.6 %add_convert_fusion.2 = bf16[256,768]{1,0:T(8,128)(2,1)S(1)} fusion(f32[256,768]{1,0:T(8,128)S(1)} %copy.51, f32[256,768]{1,0:T(8,128)S(1)} %get-tuple-element.368, f32[768]{0:T(1024)} %get-tuple-element.198, f32[256]{0:T(256)} %get-tuple-element.366, f32[768]{0:T(1024)} %get-tuple-element.199, f32[256]{0:T(256)} %get-tuple-element.365, ...), kind=kLoop, calls=%fused_computation.456 | loop fusion | flops 38338560 | bytes 2231296 | tf_op jit(solution)/shard_map/convert_element_type | solution.py:140
  78.7 1.9 fusion.236
  83.6 11.4 %reduce-scatter.3.cloned.1.call-start = ((), (), s32[]{:S(2)}) async-start(), calls=%async_computation.3 | async-start | bytes 3538944 | tf_op jit(solution)/shard_map/reduce_scatter | solution.py:155
  95.0 1.3 convert_element_type.529
  96.2 53.2 %all-gather.3.cloned.1.call-done = bf16[2048,768]{1,0:T(8,128)(2,1)} async-done(((bf16[256,768]{1,0:T(8,128)(2,1)}), bf16[2048,768]{1,0:T(8,128)(2,1)}) %all-gather.3.cloned.1.call-update) | async-done | bytes 3145744 | tf_op jit(solution)/shard_map/all_gather | solution.py:151
  149.4 11.6 %multiply_convert_fusion = (bf16[2048,384]{1,0:T(8,128)(2,1)S(1)}, f32[2048,384]{1,0:T(8,128)}, f32[2048,384]{1,0:T(8,128)}) fusion(f32[384]{0:T(512)} %convert_element_type.529, bf16[2048,768]{1,0:T(8,128)(2,1)} %all-gather.3.cloned.1.call-done, bf16[768,384]{1,0:T(8,128)(2,1)} %param.29), kind=kOutput, calls=%fused_computation.148 | convolution fusion | flops 1259864064 | bytes 11601408 | tf_op jit(solution)/shard_map/dot_general | solution.py:152
  161.0 1.2 copy-done.123
  162.2 3.4 convolution_convert_fusion.1
  165.7 1.3 convert_element_type.533
  166.9 1.3 convert_element_type.534
  168.2 1.3 convert_element_type.535
  169.5 72.7 %reduce-scatter.3.cloned.1.call-done = bf16[256,768]{1,0:T(8,128)(2,1)} async-done(((bf16[2048,768]{1,0:T(8,128)(2,1)}), bf16[256,768]{1,0:T(8,128)(2,1)}) %reduce-scatter.3.cloned.1.call-update) | async-done | bytes 393232 | tf_op jit(solution)/shard_map/reduce_scatter | solution.py:155
  242.2 1.4 fusion.233
  243.9 1.9 fusion.26
  247.8 1.5 convert_reduce_fusion.1
  249.4 62.5 %all-gather.5.cloned.1.call-done = bf16[2048,768]{1,0:T(8,128)(2,1)} async-done(((bf16[256,768]{1,0:T(8,128)(2,1)}), bf16[2048,768]{1,0:T(8,128)(2,1)}) %all-gather.5.cloned.1.call-update) | async-done | bytes 3145744 | tf_op jit(solution)/shard_map/all_gather | solution.py:167
  311.9 7.3 %fusion.230 = (bf16[384]{0:T(512)(128)(2,1)}, bf16[2048,384]{1,0:T(8,128)(2,1)S(1)}) fusion(f32[2048,384]{1,0:T(8,128)} %get-tuple-element.299, f32[2048,384]{1,0:T(8,128)} %get-tuple-element.373, bf16[2048,768]{1,0:T(8,128)(2,1)} %all-gather.5.cloned.1.call-done, bf16[384,768]{1,0:T(8,128)(2,1)} %param.31), kind=kOutput, calls=%fused_computation.674 | convolution fusion | flops 1219755648 | bytes 11600640 | tf_op jit(solution)/shard_map/dot_general | solution.py:13
  320.4 3.5 convolution_convert_fusion
  324.0 4.8 convolution_convert_fusion.2
  328.8 2.6 convolution_convert_fusion.3
  331.5 69.1 %reduce-scatter.5.cloned.1.call-done = bf16[256,768]{1,0:T(8,128)(2,1)} async-done(((bf16[2048,768]{1,0:T(8,128)(2,1)}), bf16[256,768]{1,0:T(8,128)(2,1)}) %reduce-scatter.5.cloned.1.call-update) | async-done | bytes 393232 | tf_op jit(solution)/shard_map/reduce_scatter | solution.py:173
  400.6 2.4 multiply_reduce_fusion
  403.6 1.8 fusion.231
  406.3 1.2 multiply_reduce_fusion.64
  407.5 1.9 fusion.237
  409.4 1.1 copy.52
  410.8 3.0 multiply_reduce_fusion.46
  413.8 2.9 multiply_reduce_fusion.37
  416.8 2.1 multiply_reduce_fusion.19
  419.0 2.1 multiply_reduce_fusion.10
  421.3 2.9 multiply_reduce_fusion.1
  424.3 2.1 multiply_reduce_fusion.28
  426.5 2.2 multiply_reduce_fusion.55
  429.3 1.3 fusion.222
  430.6 1.4 copy.53
  451.9 5.8 stack.263
  457.7 11.7 %convert_reduce_fusion.3 = (f32[768]{0:T(1024)S(1)}, bf16[256,768]{1,0:T(8,128)(2,1)S(1)}) fusion(f32[256]{0:T(256)} %copy-done.110, f32[256,768]{1,0:T(8,128)S(1)} %copy.53, f32[768]{0:T(1024)} %get-tuple-element.198, f32[256]{0:T(256)} %get-tuple-element.303, f32[768]{0:T(1024)} %get-tuple-element.199, f32[256]{0:T(256)} %get-tuple-element.321, ...), kind=kLoop, calls=%fused_computation.446 | loop fusion | flops 38927616 | bytes 2235392 | tf_op jit(solution)/shard_map/reduce_sum | solution.py:191
  469.4 1.9 convolution_bitcast_fusion
  472.0 28.5 %psum.99 = bf16[384]{0:T(512)(128)(2,1)S(1)} all-reduce(bf16[384]{0:T(512)(128)(2,1)S(1)} %copy-done.120), channel_id=1, replica_groups=mesh['dp'=16,'tensor'=8] {'dp'}, use_global_device_ids=true, to_apply=%region_94.95 | all-reduce | flops 384 | bytes 1536 | tf_op jit(solution)/shard_map/psum | solution.py:197
  501.1 22.6 %all-reduce.11.cloned.1.call-done = (bf16[768,384]{1,0:T(8,128)(2,1)}, bf16[384,768]{1,0:T(8,128)(2,1)}) async-done(((bf16[768,384]{1,0:T(8,128)(2,1)}, bf16[384,768]{1,0:T(8,128)(2,1)}), (bf16[768,384]{1,0:T(8,128)(2,1)}, bf16[384,768]{1,0:T(8,128)(2,1)})) %all-reduce.11.cloned.1.call-update) | async-done | bytes 1179664 | tf_op jit(solution)/shard_map/psum | solution.py:195
  523.7 2.2 convert_element_type.548
  525.9 2.2 convert_element_type.551
  528.0 68.4 %all-reduce.3 = (f32[768]{0:T(1024)}, f32[768]{0:T(1024)}, f32[768]{0:T(1024)}, f32[768]{0:T(1024)}, f32[768]{0:T(1024)}, /*index=5*/f32[768]{0:T(1024)}, f32[768]{0:T(1024)}) all-reduce(f32[768]{0:T(1024)S(1)} %get-tuple-element.290, f32[768]{0:T(1024)S(1)} %copy-done.37, ...), channel_id=1, replica_groups=mesh['dp'=16,'tensor'=8] {'dp','tensor'}, use_global_device_ids=true, to_apply=%region_18.19 | all-reduce | flops 5376 | bytes 43008 | tf_op jit(solution)/shard_map/psum | solution.py:210
  596.5 1.4 convolution_add_fusion.1
  597.9 89.3 %all-reduce.9.cloned.1.call-done = (f32[768,768]{0,1:T(8,128)}, f32[65,768]{1,0:T(8,128)}, f32[768,768]{1,0:T(8,128)}) async-done(((f32[768,768]{0,1:T(8,128)}, f32[65,768]{1,0:T(8,128)}, f32[768,768]{1,0:T(8,128)}), (f32[768,768]{0,1:T(8,128)}, f32[65,768]{1,0:T(8,128)}, f32[768,768]{1,0:T(8,128)})) %all-reduce.9.cloned.1.call-update) | async-done | bytes 4918288 | tf_op jit(solution)/shard_map/psum | solution.py:210
  687.1 3.1 copy.54
  690.9 3.2 copy.70
  (373 shorter events, 40.7 us)
Async XLA Ops:
  7.2 53.3 %copy-start = (bf16[768,768]{1,0:T(8,128)(2,1)S(1)}, bf16[768,768]{1,0:T(8,128)(2,1)}, u32[]{:S(2)}) copy-start(bf16[768,768]{1,0:T(8,128)(2,1)} %param.22) | copy-start | bytes 3538948
  7.2 142.2 %all-gather.3.cloned.1.call-start = ((), (), s32[]{:S(2)}) async-start(), calls=%async_computation.2 | async-start | bytes 3538944 | tf_op jit(solution)/shard_map/all_gather | solution.py:151
  17.3 43.1 %copy-start.119 = (s32[256]{0:T(256)S(1)}, s32[256]{0:T(256)}, u32[]{:S(2)}) copy-start(s32[256]{0:T(256)} %param.37) | copy-start | bytes 3076
  17.3 43.1 %copy-start.116 = (bf16[768]{0:T(1024)(128)(2,1)S(1)}, bf16[768]{0:T(1024)(128)(2,1)}, u32[]{:S(2)}) copy-start(bf16[768]{0:T(1024)(128)(2,1)} %param.23) | copy-start | bytes 4612
  17.3 43.1 %copy-start.6 = (bf16[256,768]{1,0:T(8,128)(2,1)S(1)}, bf16[256,768]{1,0:T(8,128)(2,1)}, u32[]{:S(2)}) copy-start(bf16[256,768]{1,0:T(8,128)(2,1)} %param.21) | copy-start | bytes 1179652
  65.6 15.8 %copy-start.117 = (bf16[768]{0:T(1024)(128)(2,1)S(1)}, bf16[768]{0:T(1024)(128)(2,1)}, u32[]{:S(2)}) copy-start(bf16[768]{0:T(1024)(128)(2,1)} %param.27) | copy-start | bytes 4612
  65.6 15.8 %copy-start.118 = (bf16[768]{0:T(1024)(128)(2,1)S(1)}, bf16[768]{0:T(1024)(128)(2,1)}, u32[]{:S(2)}) copy-start(bf16[768]{0:T(1024)(128)(2,1)} %param.28) | copy-start | bytes 4612
  83.6 158.7 %reduce-scatter.3.cloned.1.call-start = ((), (), s32[]{:S(2)}) async-start(), calls=%async_computation.3 | async-start | bytes 3538944 | tf_op jit(solution)/shard_map/reduce_scatter | solution.py:155
  149.4 12.8 %copy-start.121 = (bf16[384,768]{1,0:T(8,128)(2,1)S(1)}, bf16[384,768]{1,0:T(8,128)(2,1)}, u32[]{:S(2)}) copy-start(bf16[384,768]{1,0:T(8,128)(2,1)} %param.31) | copy-start | bytes 1769476
  165.6 146.3 %all-gather.5.cloned.1.call-start = ((), (), s32[]{:S(2)}) async-start(), calls=%async_computation.4 | async-start | bytes 3538944 | tf_op jit(solution)/shard_map/all_gather | solution.py:167
  249.3 151.3 %reduce-scatter.5.cloned.1.call-start = ((), (), s32[]{:S(2)}) async-start(), calls=%async_computation.5 | async-start | bytes 3538944 | tf_op jit(solution)/shard_map/reduce_scatter | solution.py:173
  323.9 199.8 %all-reduce.11.cloned.1.call-start = ((), (), s32[]{:S(2)}) async-start(), calls=%async_computation.7 | async-start | bytes 2359296 | tf_op jit(solution)/shard_map/psum | solution.py:195
  331.4 355.7 %all-reduce.9.cloned.1.call-start = ((), (), s32[]{:S(2)}) async-start(), calls=%async_computation.6 | async-start | bytes 9879552 | tf_op jit(solution)/shard_map/psum | solution.py:210
  410.7 10.5 %copy-start.76 = (f32[256]{0:T(256)S(1)}, f32[256]{0:T(256)}, u32[]{:S(2)}) copy-start(f32[256]{0:T(256)} %get-tuple-element.304) | copy-start | bytes 3076
  410.7 10.5 %copy-start.77 = (f32[256]{0:T(256)S(1)}, f32[256]{0:T(256)}, u32[]{:S(2)}) copy-start(f32[256]{0:T(256)} %get-tuple-element.305) | copy-start | bytes 3076
  410.7 10.5 %copy-start.78 = (f32[256]{0:T(256)S(1)}, f32[256]{0:T(256)}, u32[]{:S(2)}) copy-start(f32[256]{0:T(256)} %get-tuple-element.306) | copy-start | bytes 3076
  410.7 10.5 %copy-start.79 = (f32[256]{0:T(256)S(1)}, f32[256]{0:T(256)}, u32[]{:S(2)}) copy-start(f32[256]{0:T(256)} %get-tuple-element.307) | copy-start | bytes 3076
  410.7 10.4 %copy-start.80 = (f32[256]{0:T(256)S(1)}, f32[256]{0:T(256)}, u32[]{:S(2)}) copy-start(f32[256]{0:T(256)} %get-tuple-element.308) | copy-start | bytes 3076
  428.9 20.9 %copy-start.73 = (f32[768]{0:T(1024)S(1)}, f32[768]{0:T(1024)}, u32[]{:S(2)}) copy-start(f32[768]{0:T(1024)} %get-tuple-element.145) | copy-start | bytes 9220
  428.9 20.9 %copy-start.72 = (f32[768]{0:T(1024)S(1)}, f32[768]{0:T(1024)}, u32[]{:S(2)}) copy-start(f32[768]{0:T(1024)} %get-tuple-element.144) | copy-start | bytes 9220
  428.9 20.9 %copy-start.71 = (f32[768]{0:T(1024)S(1)}, f32[768]{0:T(1024)}, u32[]{:S(2)}) copy-start(f32[768]{0:T(1024)} %get-tuple-element.143) | copy-start | bytes 9220
  428.9 20.9 %copy-start.70 = (f32[768]{0:T(1024)S(1)}, f32[768]{0:T(1024)}, u32[]{:S(2)}) copy-start(f32[768]{0:T(1024)} %get-tuple-element.142) | copy-start | bytes 9220
  428.9 20.9 %copy-start.69 = (f32[768]{0:T(1024)S(1)}, f32[768]{0:T(1024)}, u32[]{:S(2)}) copy-start(f32[768]{0:T(1024)} %get-tuple-element.141) | copy-start | bytes 9220
  428.9 20.9 %copy-start.68 = (f32[768]{0:T(1024)S(1)}, f32[768]{0:T(1024)}, u32[]{:S(2)}) copy-start(f32[768]{0:T(1024)} %get-tuple-element.140) | copy-start | bytes 9220
  428.9 20.9 %copy-start.67 = (f32[768]{0:T(1024)S(1)}, f32[768]{0:T(1024)}, u32[]{:S(2)}) copy-start(f32[768]{0:T(1024)} %get-tuple-element.139) | copy-start | bytes 9220
  428.9 20.9 %copy-start.66 = (f32[768]{0:T(1024)S(1)}, f32[768]{0:T(1024)}, u32[]{:S(2)}) copy-start(f32[768]{0:T(1024)} %get-tuple-element.138) | copy-start | bytes 9220
  428.9 21.0 %copy-start.65 = (f32[768]{0:T(1024)S(1)}, f32[768]{0:T(1024)}, u32[]{:S(2)}) copy-start(f32[768]{0:T(1024)} %get-tuple-element.137) | copy-start | bytes 9220
  429.0 21.0 %copy-start.64 = (f32[768]{0:T(1024)S(1)}, f32[768]{0:T(1024)}, u32[]{:S(2)}) copy-start(f32[768]{0:T(1024)} %get-tuple-element.136) | copy-start | bytes 9220
  429.0 21.0 %copy-start.63 = (f32[768]{0:T(1024)S(1)}, f32[768]{0:T(1024)}, u32[]{:S(2)}) copy-start(f32[768]{0:T(1024)} %get-tuple-element.135) | copy-start | bytes 9220
  429.0 21.0 %copy-start.62 = (f32[768]{0:T(1024)S(1)}, f32[768]{0:T(1024)}, u32[]{:S(2)}) copy-start(f32[768]{0:T(1024)} %get-tuple-element.134) | copy-start | bytes 9220
  429.0 21.0 %copy-start.61 = (f32[768]{0:T(1024)S(1)}, f32[768]{0:T(1024)}, u32[]{:S(2)}) copy-start(f32[768]{0:T(1024)} %get-tuple-element.133) | copy-start | bytes 9220
  429.0 21.0 %copy-start.60 = (f32[768]{0:T(1024)S(1)}, f32[768]{0:T(1024)}, u32[]{:S(2)}) copy-start(f32[768]{0:T(1024)} %get-tuple-element.132) | copy-start | bytes 9220
  429.0 21.0 %copy-start.59 = (f32[768]{0:T(1024)S(1)}, f32[768]{0:T(1024)}, u32[]{:S(2)}) copy-start(f32[768]{0:T(1024)} %get-tuple-element.131) | copy-start | bytes 9220
  429.0 21.0 %copy-start.58 = (f32[768]{0:T(1024)S(1)}, f32[768]{0:T(1024)}, u32[]{:S(2)}) copy-start(f32[768]{0:T(1024)} %get-tuple-element.130) | copy-start | bytes 9220
  429.0 21.0 %copy-start.57 = (f32[768]{0:T(1024)S(1)}, f32[768]{0:T(1024)}, u32[]{:S(2)}) copy-start(f32[768]{0:T(1024)} %get-tuple-element.129) | copy-start | bytes 9220
  429.0 21.1 %copy-start.56 = (f32[768]{0:T(1024)S(1)}, f32[768]{0:T(1024)}, u32[]{:S(2)}) copy-start(f32[768]{0:T(1024)} %get-tuple-element.128) | copy-start | bytes 9220
  429.0 21.1 %copy-start.55 = (f32[768]{0:T(1024)S(1)}, f32[768]{0:T(1024)}, u32[]{:S(2)}) copy-start(f32[768]{0:T(1024)} %get-tuple-element.163) | copy-start | bytes 9220
  429.1 21.1 %copy-start.54 = (f32[768]{0:T(1024)S(1)}, f32[768]{0:T(1024)}, u32[]{:S(2)}) copy-start(f32[768]{0:T(1024)} %get-tuple-element.162) | copy-start | bytes 9220
  429.1 21.1 %copy-start.53 = (f32[768]{0:T(1024)S(1)}, f32[768]{0:T(1024)}, u32[]{:S(2)}) copy-start(f32[768]{0:T(1024)} %get-tuple-element.161) | copy-start | bytes 9220
  429.1 21.1 %copy-start.52 = (f32[768]{0:T(1024)S(1)}, f32[768]{0:T(1024)}, u32[]{:S(2)}) copy-start(f32[768]{0:T(1024)} %get-tuple-element.160) | copy-start | bytes 9220
  429.1 21.1 %copy-start.51 = (f32[768]{0:T(1024)S(1)}, f32[768]{0:T(1024)}, u32[]{:S(2)}) copy-start(f32[768]{0:T(1024)} %get-tuple-element.159) | copy-start | bytes 9220
  429.1 21.1 %copy-start.50 = (f32[768]{0:T(1024)S(1)}, f32[768]{0:T(1024)}, u32[]{:S(2)}) copy-start(f32[768]{0:T(1024)} %get-tuple-element.158) | copy-start | bytes 9220
  429.1 21.1 %copy-start.49 = (f32[768]{0:T(1024)S(1)}, f32[768]{0:T(1024)}, u32[]{:S(2)}) copy-start(f32[768]{0:T(1024)} %get-tuple-element.157) | copy-start | bytes 9220
  429.1 21.2 %copy-start.48 = (f32[768]{0:T(1024)S(1)}, f32[768]{0:T(1024)}, u32[]{:S(2)}) copy-start(f32[768]{0:T(1024)} %get-tuple-element.156) | copy-start | bytes 9220
  429.1 21.2 %copy-start.47 = (f32[768]{0:T(1024)S(1)}, f32[768]{0:T(1024)}, u32[]{:S(2)}) copy-start(f32[768]{0:T(1024)} %get-tuple-element.155) | copy-start | bytes 9220
  429.1 21.2 %copy-start.46 = (f32[768]{0:T(1024)S(1)}, f32[768]{0:T(1024)}, u32[]{:S(2)}) copy-start(f32[768]{0:T(1024)} %get-tuple-element.190) | copy-start | bytes 9220
  429.1 21.2 %copy-start.45 = (f32[768]{0:T(1024)S(1)}, f32[768]{0:T(1024)}, u32[]{:S(2)}) copy-start(f32[768]{0:T(1024)} %get-tuple-element.189) | copy-start | bytes 9220
  429.2 21.2 %copy-start.44 = (f32[768]{0:T(1024)S(1)}, f32[768]{0:T(1024)}, u32[]{:S(2)}) copy-start(f32[768]{0:T(1024)} %get-tuple-element.188) | copy-start | bytes 9220
  429.2 21.2 %copy-start.43 = (f32[768]{0:T(1024)S(1)}, f32[768]{0:T(1024)}, u32[]{:S(2)}) copy-start(f32[768]{0:T(1024)} %get-tuple-element.187) | copy-start | bytes 9220
  429.2 21.2 %copy-start.42 = (f32[768]{0:T(1024)S(1)}, f32[768]{0:T(1024)}, u32[]{:S(2)}) copy-start(f32[768]{0:T(1024)} %get-tuple-element.186) | copy-start | bytes 9220
  429.2 21.2 %copy-start.41 = (f32[768]{0:T(1024)S(1)}, f32[768]{0:T(1024)}, u32[]{:S(2)}) copy-start(f32[768]{0:T(1024)} %get-tuple-element.185) | copy-start | bytes 9220
  429.2 21.3 %copy-start.40 = (f32[768]{0:T(1024)S(1)}, f32[768]{0:T(1024)}, u32[]{:S(2)}) copy-start(f32[768]{0:T(1024)} %get-tuple-element.184) | copy-start | bytes 9220
  429.2 21.3 %copy-start.39 = (f32[768]{0:T(1024)S(1)}, f32[768]{0:T(1024)}, u32[]{:S(2)}) copy-start(f32[768]{0:T(1024)} %get-tuple-element.183) | copy-start | bytes 9220
  429.2 21.3 %copy-start.38 = (f32[768]{0:T(1024)S(1)}, f32[768]{0:T(1024)}, u32[]{:S(2)}) copy-start(f32[768]{0:T(1024)} %get-tuple-element.182) | copy-start | bytes 9220
  429.3 20.5 %copy-start.74 = (f32[768]{0:T(1024)S(1)}, f32[768]{0:T(1024)}, u32[]{:S(2)}) copy-start(f32[768]{0:T(1024)} %get-tuple-element.146) | copy-start | bytes 9220
  430.6 38.8 %copy-start.7 = (bf16[256,768]{1,0:T(8,128)(2,1)S(1)}, bf16[256,768]{1,0:T(8,128)(2,1)}, u32[]{:S(2)}) copy-start(bf16[256,768]{1,0:T(8,128)(2,1)} %param.21) | copy-start | bytes 1179652
  471.3 56.7 %copy-start.32 = (f32[768]{0:T(1024)S(1)}, f32[768]{0:T(1024)}, u32[]{:S(2)}) copy-start(f32[768]{0:T(1024)} %get-tuple-element.193) | copy-start | bytes 9220
  471.3 56.7 %copy-start.33 = (f32[768]{0:T(1024)S(1)}, f32[768]{0:T(1024)}, u32[]{:S(2)}) copy-start(f32[768]{0:T(1024)} %get-tuple-element.196) | copy-start | bytes 9220
  471.3 56.7 %copy-start.34 = (f32[768]{0:T(1024)S(1)}, f32[768]{0:T(1024)}, u32[]{:S(2)}) copy-start(f32[768]{0:T(1024)} %get-tuple-element.286) | copy-start | bytes 9220
  471.3 56.7 %copy-start.35 = (f32[768]{0:T(1024)S(1)}, f32[768]{0:T(1024)}, u32[]{:S(2)}) copy-start(f32[768]{0:T(1024)} %get-tuple-element.126) | copy-start | bytes 9220
  471.3 56.7 %copy-start.36 = (f32[768]{0:T(1024)S(1)}, f32[768]{0:T(1024)}, u32[]{:S(2)}) copy-start(f32[768]{0:T(1024)} %get-tuple-element.195) | copy-start | bytes 9220
  471.4 56.7 %copy-start.37 = (f32[768]{0:T(1024)S(1)}, f32[768]{0:T(1024)}, u32[]{:S(2)}) copy-start(f32[768]{0:T(1024)} %get-tuple-element.288) | copy-start | bytes 9220
  471.4 125.1 %copy-start.3 = (f32[256,768]{1,0:T(8,128)S(1)}, f32[256,768]{1,0:T(8,128)}, u32[]{:S(2)}) copy-start(f32[256,768]{1,0:T(8,128)} %copy-done.2) | copy-start | bytes 2359300
  471.4 125.1 %copy-start.115 = (f32[256]{0:T(256)S(1)}, f32[256]{0:T(256)}, u32[]{:S(2)}) copy-start(f32[256]{0:T(256)} %copy-done.114) | copy-start | bytes 3076
  (66 other events, 390.9 us)
Sparse Core Ops, SparseCore 0:
  83.7 65.6 all-gather.2
  165.7 76.4 reduce-scatter.2
  249.5 62.4 all-gather.4
  324.0 76.5 reduce-scatter.4
  403.6 120.0 all-reduce.10
  529.7 157.4 all-reduce.8
where the time goes:
time: 710 us; the launch traced here: 701 us
  waiting for transfers between devices  369 us (52%)
  blocking collectives  97 us (14%)
  matrix products  88.4 us (12%)
  other arithmetic  70.4 us (10%)
  local copies, waits for them, and re-layouts  48.2 us (7%)
  between operations  16.4 us (2%)
  starting transfers between devices  11.6 us (2%)
    psum x1, waiting for transfers between devices, body(): lax.psum((grad_w_value, grad_b_value, grad_kernel, grad_w_out, grad_b_out...  89.3 us
    reduce_scatter x1, waiting for transfers between devices, body(): lax.psum_scatter(jnp.dot(active, w_down, preferred_element_type=jnp.float...  72.7 us
    reduce_scatter x1, waiting for transfers between devices, body(): lax.psum_scatter(dot_last(upper_grad, w_up).astype(jnp.bfloat16), 'tensor...  69.1 us
    psum x1, blocking collectives, body(): lax.psum((grad_w_value, grad_b_value, grad_kernel, grad_w_out, grad_b_out...  68.4 us
    all_gather x1, waiting for transfers between devices, body(): grad_rows_all = lax.all_gather(branch_grad, 'tensor', axis=0, tiled=True)  62.5 us
    dot_general x16, matrix products, dot_last(): lax.dot_general(former, latter, (((1,), (1,)), ((), ())), preferred_eleme...  56.4 us
    all_gather x1, waiting for transfers between devices, body(): gathered = lax.all_gather(first_low, 'tensor', axis=0, tiled=True)  53.2 us
    psum x1, blocking collectives, body(): lax.psum(grad_b_up.astype(jnp.bfloat16), 'dp').astype(jnp.float32)  28.5 us
  transfers between devices with their start and end apart: 6, of which 6 were waited for; matrix products, arithmetic and copies ran while one was open for 12% of the time, Pallas kernels for 0%

commit v1 on v0

--- a/solution.py
+++ b/solution.py
@@ -7,6 +7,13 @@
 HEADS = 12
 SETS = 32
 BUCKETS = 256
+
+
+def exchange_gather(x, mesh_axis, along):
+    size = lax.axis_size(mesh_axis)
+    tiles = jnp.stack([x for _ in range(size)])
+    tiles = lax.all_to_all(tiles, mesh_axis, split_axis=0, concat_axis=0)
+    return jnp.concatenate(tiles, axis=along)
 
 
 def dot_last(former, latter):
@@ -164,7 +171,7 @@
     grad_second, grad_gain_ffn, grad_shift_ffn = second_back(out_grad.astype(jnp.float32))
     branch_grad = grad_second.astype(jnp.bfloat16)
     grad_b_down = jnp.sum(branch_grad.astype(jnp.float32), axis=0)
-    grad_rows_all = lax.all_gather(branch_grad, "tensor", axis=0, tiled=True)
+    grad_rows_all = exchange_gather(branch_grad, "tensor", 0)
     active_grad = dot_last(grad_rows_all, w_down)
     grad_w_down = dot_first(active, grad_rows_all)
     upper_grad = gelu_back(active_grad)[0].astype(jnp.bfloat16)

time: 710 us -> 690 us (0.972)
  waiting for transfers between devices: 369 us -> 268 us
  local copies, waits for them, and re-layouts: 48.2 us -> 91.6 us
  blocking collectives: 97 us -> 133 us
    all_gather x1 -> x0, waiting for transfers between devices: 62.5 us -> none  [body(): grad_rows_all = lax.all_gather(branch_grad, 'tensor', axis=0, tiled=True)]
    another operation x66, local copies, waits for them, and re-layouts: 25 us -> 68.8 us  [conv_back(): return (value_grad, jnp.stack(tap_rows, axis=0))]
    all_to_all x0 -> x1, blocking collectives: none -> 39.9 us  [exchange_gather(): tiles = lax.all_to_all(tiles, mesh_axis, split_axis=0, concat_axis=0)]
    psum x1, waiting for transfers between devices: 22.6 us -> 0.01 us  [body(): lax.psum(grad_w_up.astype(jnp.bfloat16), 'dp').astype(jnp.float32)]
    psum x1, waiting for transfers between devices: 89.3 us -> 69.9 us  [body(): lax.psum((grad_w_value, grad_b_value, grad_kernel, grad_w_out, grad_b_out...]
    unnamed x253 -> x263, local copies, waits for them, and re-layouts: 16.1 us -> 15.4 us
  transfers between devices with their start and end apart: 6 -> 5, of which waited for: 6 -> 4; matrix products, arithmetic and copies ran while one was open for 12% -> 19% of each run, Pallas kernels for 0% -> 0%
where the time goes in v1:
time: 690 us; the launch traced here: 681 us
  waiting for transfers between devices  268 us (39%)
  blocking collectives  133 us (19%)
  local copies, waits for them, and re-layouts  91.6 us (13%)
  matrix products  86.6 us (13%)
  other arithmetic  74.5 us (11%)
  between operations  15.6 us (2%)
  starting transfers between devices  11.4 us (2%)
    reduce_scatter x1, waiting for transfers between devices, body(): lax.psum_scatter(jnp.dot(active, w_down, preferred_element_type=jnp.float...  72.8 us
    reduce_scatter x1, waiting for transfers between devices, body(): lax.psum_scatter(dot_last(upper_grad, w_up).astype(jnp.bfloat16), 'tensor...  72.1 us
    psum x1, waiting for transfers between devices, body(): lax.psum((grad_w_value, grad_b_value, grad_kernel, grad_w_out, grad_b_out...  69.9 us
    another operation x66, local copies, waits for them, and re-layouts, conv_back(): return (value_grad, jnp.stack(tap_rows, axis=0))  68.8 us
    psum x1, blocking collectives, body(): lax.psum((grad_w_value, grad_b_value, grad_kernel, grad_w_out, grad_b_out...  65.3 us
    all_gather x1, waiting for transfers between devices, body(): gathered = lax.all_gather(first_low, 'tensor', axis=0, tiled=True)  53.3 us
    dot_general x16, matrix products, dot_last(): lax.dot_general(former, latter, (((1,), (1,)), ((), ())), preferred_eleme...  52.4 us
    all_to_all x1, blocking collectives, exchange_gather(): tiles = lax.all_to_all(tiles, mesh_axis, split_axis=0, concat_axis=0)  39.9 us
  transfers between devices with their start and end apart: 5, of which 4 were waited for; matrix products, arithmetic and copies ran while one was open for 19% of the time, Pallas kernels for 0%

profile of v1, /device:TPU:1, one launch (start us, length us, event | category | flops | bytes accessed | tf_op | source)
XLA Modules:
  0.0 681.4 jit_solution(15733315069290165663)
XLA Ops:
  15.6 1.3 convert_element_type.526
  16.9 1.3 convert_element_type.527
  18.9 1.3 convert_element_type.525
  22.5 1.5 fusion.235
  24.1 43.1 %while.12 = (s32[]{:T(128)}, bf16[12,256,256]{2,1,0:T(8,128)(2,1)}, s32[12,256,32]{1,2,0:T(8,128)S(1)}, s32[12,256,32]{1,2,0:T(8,128)S(1)}, s32[256]{0:T(256)S(1)}, /*index=5*/s32[]{:T(128)}) while((s32[]{:T(128)}, bf16[12,256,256]{2,1,0:T(8,128)(2,1)}, s32[12,256,32]{1,2,0:T(8,128)S(1)}, s32[12,256,32]{1,2,0:T(8,128)S(1)}, ...), condition=%wide.region_3.4_spmd.clone.clone, body=%wide.region_2.3_spmd.clone.clone.sunk | while | flops 1078198272 | bytes 329813 | solution.py:132
  24.2 3.6 fusion.266
  27.8 3.6 fusion.266
  31.4 3.6 fusion.266
  34.9 3.6 fusion.266
  38.5 3.6 fusion.266
  42.1 3.6 fusion.266
  45.7 3.6 fusion.266
  49.3 3.6 fusion.266
  52.9 3.6 fusion.266
  56.5 3.6 fusion.266
  60.1 3.6 fusion.266
  63.6 3.6 fusion.266
  67.2 2.0 multiply_reduce_fusion.70
  70.2 1.4 copy.51
  71.6 12.1 %add_convert_fusion.2 = bf16[256,768]{1,0:T(8,128)(2,1)S(1)} fusion(f32[256,768]{1,0:T(8,128)S(1)} %copy.51, f32[256,768]{1,0:T(8,128)S(1)} %get-tuple-element.368, f32[768]{0:T(1024)} %get-tuple-element.198, f32[256]{0:T(256)} %get-tuple-element.366, f32[768]{0:T(1024)} %get-tuple-element.199, f32[256]{0:T(256)} %get-tuple-element.365, ...), kind=kLoop, calls=%fused_computation.456 | loop fusion | flops 38338560 | bytes 2231296 | tf_op jit(solution)/shard_map/convert_element_type | solution.py:147
  84.5 1.9 fusion.236
  88.8 11.2 %reduce-scatter.3.cloned.1.call-start = ((), (), s32[]{:S(2)}) async-start(), calls=%async_computation.4 | async-start | bytes 3538944 | tf_op jit(solution)/shard_map/reduce_scatter | solution.py:162
  101.3 53.3 %all-gather.2.cloned.1.call-done = bf16[2048,768]{1,0:T(8,128)(2,1)} async-done(((bf16[256,768]{1,0:T(8,128)(2,1)}), bf16[2048,768]{1,0:T(8,128)(2,1)}) %all-gather.2.cloned.1.call-update) | async-done | bytes 3145744 | tf_op jit(solution)/shard_map/all_gather | solution.py:158
  154.6 11.6 %multiply_convert_fusion = (bf16[2048,384]{1,0:T(8,128)(2,1)S(1)}, f32[2048,384]{1,0:T(8,128)}, f32[2048,384]{1,0:T(8,128)}) fusion(f32[384]{0:T(512)} %convert_element_type.529, bf16[2048,768]{1,0:T(8,128)(2,1)} %all-gather.2.cloned.1.call-done, bf16[768,384]{1,0:T(8,128)(2,1)} %param.29), kind=kOutput, calls=%fused_computation.148 | convolution fusion | flops 1259864064 | bytes 11601408 | tf_op jit(solution)/shard_map/dot_general | solution.py:159
  167.4 3.4 convolution_convert_fusion.1
  170.9 1.3 convert_element_type.534
  172.2 1.3 convert_element_type.533
  173.5 1.3 convert_element_type.535
  174.7 72.8 %reduce-scatter.3.cloned.1.call-done = bf16[256,768]{1,0:T(8,128)(2,1)} async-done(((bf16[2048,768]{1,0:T(8,128)(2,1)}), bf16[256,768]{1,0:T(8,128)(2,1)}) %reduce-scatter.3.cloned.1.call-update) | async-done | bytes 393232 | tf_op jit(solution)/shard_map/reduce_scatter | solution.py:162
  247.5 1.4 fusion.233
  249.1 1.9 fusion.26
  253.3 39.9 %all_to_all.5 = bf16[8,256,768]{2,1,0:T(8,128)(2,1)S(1)} all-to-all(bf16[8,256,768]{2,1,0:T(8,128)(2,1)S(1)} %stack.209), channel_id=1, replica_groups=mesh['dp'=16,'tensor'=8] {'tensor'}, dimensions={0} | all-to-all | bytes 6291456 | tf_op jit(solution)/shard_map/all_to_all | solution.py:15
  293.3 3.3 fusion.230
  297.8 3.5 convolution_convert_fusion
  301.4 4.7 convolution_convert_fusion.2
  306.2 2.6 convolution_convert_fusion.3
  308.9 72.1 %reduce-scatter.5.cloned.1.call-done = bf16[256,768]{1,0:T(8,128)(2,1)} async-done(((bf16[2048,768]{1,0:T(8,128)(2,1)}), bf16[256,768]{1,0:T(8,128)(2,1)}) %reduce-scatter.5.cloned.1.call-update) | async-done | bytes 393232 | tf_op jit(solution)/shard_map/reduce_scatter | solution.py:180
  381.0 2.4 multiply_reduce_fusion
  384.1 1.7 fusion.231
  388.8 2.3 multiply_reduce_fusion.19
  391.3 2.7 multiply_reduce_fusion.55
  394.2 2.8 multiply_reduce_fusion.37
  397.0 2.9 multiply_reduce_fusion.46
  399.9 2.1 multiply_reduce_fusion.10
  402.1 2.1 multiply_reduce_fusion.28
  404.3 2.1 multiply_reduce_fusion.1
  407.0 3.2 fusion.237
  410.2 1.3 stack.211
  416.5 1.3 stack.253
  434.3 1.3 stack.212
  443.1 1.3 stack.232
  467.1 1.3 fusion.222
  468.4 2.3 copy.53
  470.8 12.2 %stack.275 = f32[65,768]{1,0:T(8,128)} concatenate(f32[1,768]{1,0:T(1,128)} %stack.210, f32[1,768]{1,0:T(1,128)} %stack.211, f32[1,768]{1,0:T(1,128)} %stack.212, f32[1,768]{1,0:T(1,128)} %stack.213, f32[1,768]{1,0:T(1,128)} %stack.214, f32[1,768]{1,0:T(1,128)} %stack.215, f32[1,768]{1,0:T(1,128)} %stack.216, f32[1,768]{1,0:T(1,128)} %stack.217, f32[1,768]{1,0:T(1,128)} %stack.218, ...), dimensions={0} | concatenate | bytes 399360 | tf_op jit(solution)/shard_map/stack | solution.py:79
  483.0 12.0 %convert_reduce_fusion.3 = (f32[768]{0:T(1024)S(1)}, bf16[256,768]{1,0:T(8,128)(2,1)S(1)}) fusion(f32[256]{0:T(256)} %copy-done.116, f32[256,768]{1,0:T(8,128)} %copy.53, f32[768]{0:T(1024)} %get-tuple-element.198, f32[256]{0:T(256)} %get-tuple-element.303, f32[768]{0:T(1024)} %get-tuple-element.199, f32[256]{0:T(256)} %get-tuple-element.321, ...), kind=kLoop, calls=%fused_computation.446 | loop fusion | flops 38927616 | bytes 2235392 | tf_op jit(solution)/shard_map/reduce_sum | solution.py:198
  495.0 1.9 convolution_bitcast_fusion
  497.6 28.3 %psum.99 = bf16[384]{0:T(512)(128)(2,1)S(1)} all-reduce(bf16[384]{0:T(512)(128)(2,1)S(1)} %copy-done.122), channel_id=1, replica_groups=mesh['dp'=16,'tensor'=8] {'dp'}, use_global_device_ids=true, to_apply=%region_94.95 | all-reduce | flops 384 | bytes 1536 | tf_op jit(solution)/shard_map/psum | solution.py:204
  526.4 2.2 convert_element_type.548
  528.6 2.2 convert_element_type.551
  530.8 65.3 %all-reduce.3 = (f32[768]{0:T(1024)}, f32[768]{0:T(1024)}, f32[768]{0:T(1024)}, f32[768]{0:T(1024)}, f32[768]{0:T(1024)}, /*index=5*/f32[768]{0:T(1024)}, f32[768]{0:T(1024)}) all-reduce(f32[768]{0:T(1024)S(1)} %get-tuple-element.290, f32[768]{0:T(1024)S(1)} %copy-done.36, ...), channel_id=1, replica_groups=mesh['dp'=16,'tensor'=8] {'dp','tensor'}, use_global_device_ids=true, to_apply=%region_18.19 | all-reduce | flops 5376 | bytes 43008 | tf_op jit(solution)/shard_map/psum | solution.py:217
  596.1 1.4 convolution_add_fusion.1
  597.5 69.9 %all-reduce.9.cloned.1.call-done = (f32[768,768]{0,1:T(8,128)}, f32[65,768]{1,0:T(8,128)}, f32[768,768]{1,0:T(8,128)}) async-done(((f32[768,768]{0,1:T(8,128)}, f32[65,768]{1,0:T(8,128)}, f32[768,768]{1,0:T(8,128)}), (f32[768,768]{0,1:T(8,128)}, f32[65,768]{1,0:T(8,128)}, f32[768,768]{1,0:T(8,128)})) %all-reduce.9.cloned.1.call-update) | async-done | bytes 4918288 | tf_op jit(solution)/shard_map/psum | solution.py:217
  667.4 3.1 copy.54
  671.2 3.2 copy.70
  (382 shorter events, 79.6 us)
Async XLA Ops:
  7.2 15.3 %copy-start = (bf16[768,768]{1,0:T(8,128)(2,1)S(1)}, bf16[768,768]{1,0:T(8,128)(2,1)}, u32[]{:S(2)}) copy-start(bf16[768,768]{1,0:T(8,128)(2,1)} %param.22) | copy-start | bytes 3538948
  7.2 147.4 %all-gather.2.cloned.1.call-start = ((), (), s32[]{:S(2)}) async-start(), calls=%async_computation.3 | async-start | bytes 3538944 | tf_op jit(solution)/shard_map/all_gather | solution.py:158
  71.6 16.2 %copy-start.17 = (f32[768]{0:T(1024)S(1)}, f32[768]{0:T(1024)}, u32[]{:S(2)}) copy-start(f32[768]{0:T(1024)} %convert_element_type.526) | copy-start | bytes 9220
  71.6 16.2 %copy-start.19 = (f32[768]{0:T(1024)S(1)}, f32[768]{0:T(1024)}, u32[]{:S(2)}) copy-start(f32[768]{0:T(1024)} %convert_element_type.527) | copy-start | bytes 9220
  88.8 158.7 %reduce-scatter.3.cloned.1.call-start = ((), (), s32[]{:S(2)}) async-start(), calls=%async_computation.4 | async-start | bytes 3538944 | tf_op jit(solution)/shard_map/reduce_scatter | solution.py:162
  154.6 12.8 %copy-start.123 = (bf16[384,768]{1,0:T(8,128)(2,1)S(1)}, bf16[384,768]{1,0:T(8,128)(2,1)}, u32[]{:S(2)}) copy-start(bf16[384,768]{1,0:T(8,128)(2,1)} %param.31) | copy-start | bytes 1769476
  170.9 210.1 %reduce-scatter.5.cloned.1.call-start = ((), (), s32[]{:S(2)}) async-start(), calls=%async_computation.5 | async-start | bytes 3538944 | tf_op jit(solution)/shard_map/reduce_scatter | solution.py:180
  253.1 40.2 %copy-start.128 = (f32[2048,384]{1,0:T(8,128)S(1)}, f32[2048,384]{1,0:T(8,128)}, u32[]{:S(2)}) copy-start(f32[2048,384]{1,0:T(8,128)} %get-tuple-element.373) | copy-start | bytes 9437188
  253.3 39.9 %copy-start.124 = (bf16[384,768]{1,0:T(8,128)(2,1)S(1)}, bf16[384,768]{1,0:T(8,128)(2,1)}, u32[]{:S(2)}) copy-start(bf16[384,768]{1,0:T(8,128)(2,1)} %param.31) | copy-start | bytes 1769476
  253.3 39.9 %copy-start.127 = (f32[2048,384]{1,0:T(8,128)S(1)}, f32[2048,384]{1,0:T(8,128)}, u32[]{:S(2)}) copy-start(f32[2048,384]{1,0:T(8,128)} %get-tuple-element.299) | copy-start | bytes 9437188
  301.3 225.1 %all-reduce.11.cloned.1.call-start = ((), (), s32[]{:S(2)}) async-start(), calls=%async_computation.7 | async-start | bytes 2359296 | tf_op jit(solution)/shard_map/psum | solution.py:202
  308.8 358.6 %all-reduce.9.cloned.1.call-start = ((), (), s32[]{:S(2)}) async-start(), calls=%async_computation.6 | async-start | bytes 9879552 | tf_op jit(solution)/shard_map/psum | solution.py:217
  388.7 11.1 %copy-start.92 = (f32[256]{0:T(256)S(1)}, f32[256]{0:T(256)}, u32[]{:S(2)}) copy-start(f32[256]{0:T(256)} %get-tuple-element.311) | copy-start | bytes 3076
  388.8 11.1 %copy-start.93 = (f32[256]{0:T(256)S(1)}, f32[256]{0:T(256)}, u32[]{:S(2)}) copy-start(f32[256]{0:T(256)} %get-tuple-element.312) | copy-start | bytes 3076
  388.8 11.1 %copy-start.94 = (f32[256]{0:T(256)S(1)}, f32[256]{0:T(256)}, u32[]{:S(2)}) copy-start(f32[256]{0:T(256)} %get-tuple-element.313) | copy-start | bytes 3076
  406.6 37.8 %copy-start.74 = (f32[768]{0:T(1024)S(1)}, f32[768]{0:T(1024)}, u32[]{:S(2)}) copy-start(f32[768]{0:T(1024)} %get-tuple-element.171) | copy-start | bytes 9220
  406.6 38.4 %copy-start.73 = (f32[768]{0:T(1024)S(1)}, f32[768]{0:T(1024)}, u32[]{:S(2)}) copy-start(f32[768]{0:T(1024)} %get-tuple-element.172) | copy-start | bytes 9220
  406.6 38.9 %copy-start.72 = (f32[768]{0:T(1024)S(1)}, f32[768]{0:T(1024)}, u32[]{:S(2)}) copy-start(f32[768]{0:T(1024)} %get-tuple-element.173) | copy-start | bytes 9220
  406.6 39.5 %copy-start.71 = (f32[768]{0:T(1024)S(1)}, f32[768]{0:T(1024)}, u32[]{:S(2)}) copy-start(f32[768]{0:T(1024)} %get-tuple-element.174) | copy-start | bytes 9220
  406.7 40.1 %copy-start.70 = (f32[768]{0:T(1024)S(1)}, f32[768]{0:T(1024)}, u32[]{:S(2)}) copy-start(f32[768]{0:T(1024)} %get-tuple-element.175) | copy-start | bytes 9220
  406.7 40.7 %copy-start.69 = (f32[768]{0:T(1024)S(1)}, f32[768]{0:T(1024)}, u32[]{:S(2)}) copy-start(f32[768]{0:T(1024)} %get-tuple-element.176) | copy-start | bytes 9220
  406.7 41.3 %copy-start.68 = (f32[768]{0:T(1024)S(1)}, f32[768]{0:T(1024)}, u32[]{:S(2)}) copy-start(f32[768]{0:T(1024)} %get-tuple-element.177) | copy-start | bytes 9220
  406.7 41.9 %copy-start.67 = (f32[768]{0:T(1024)S(1)}, f32[768]{0:T(1024)}, u32[]{:S(2)}) copy-start(f32[768]{0:T(1024)} %get-tuple-element.178) | copy-start | bytes 9220
  406.7 42.5 %copy-start.66 = (f32[768]{0:T(1024)S(1)}, f32[768]{0:T(1024)}, u32[]{:S(2)}) copy-start(f32[768]{0:T(1024)} %get-tuple-element.179) | copy-start | bytes 9220
  406.7 43.0 %copy-start.65 = (f32[768]{0:T(1024)S(1)}, f32[768]{0:T(1024)}, u32[]{:S(2)}) copy-start(f32[768]{0:T(1024)} %get-tuple-element.180) | copy-start | bytes 9220
  406.7 43.6 %copy-start.63 = (f32[768]{0:T(1024)S(1)}, f32[768]{0:T(1024)}, u32[]{:S(2)}) copy-start(f32[768]{0:T(1024)} %get-tuple-element.181) | copy-start | bytes 9220
  406.7 44.2 %copy-start.62 = (f32[768]{0:T(1024)S(1)}, f32[768]{0:T(1024)}, u32[]{:S(2)}) copy-start(f32[768]{0:T(1024)} %get-tuple-element.137) | copy-start | bytes 9220
  406.7 44.8 %copy-start.61 = (f32[768]{0:T(1024)S(1)}, f32[768]{0:T(1024)}, u32[]{:S(2)}) copy-start(f32[768]{0:T(1024)} %get-tuple-element.138) | copy-start | bytes 9220
  406.7 45.4 %copy-start.60 = (f32[768]{0:T(1024)S(1)}, f32[768]{0:T(1024)}, u32[]{:S(2)}) copy-start(f32[768]{0:T(1024)} %get-tuple-element.139) | copy-start | bytes 9220
  406.8 46.0 %copy-start.59 = (f32[768]{0:T(1024)S(1)}, f32[768]{0:T(1024)}, u32[]{:S(2)}) copy-start(f32[768]{0:T(1024)} %get-tuple-element.140) | copy-start | bytes 9220
  406.8 46.6 %copy-start.58 = (f32[768]{0:T(1024)S(1)}, f32[768]{0:T(1024)}, u32[]{:S(2)}) copy-start(f32[768]{0:T(1024)} %get-tuple-element.141) | copy-start | bytes 9220
  406.8 47.1 %copy-start.57 = (f32[768]{0:T(1024)S(1)}, f32[768]{0:T(1024)}, u32[]{:S(2)}) copy-start(f32[768]{0:T(1024)} %get-tuple-element.142) | copy-start | bytes 9220
  406.8 47.7 %copy-start.56 = (f32[768]{0:T(1024)S(1)}, f32[768]{0:T(1024)}, u32[]{:S(2)}) copy-start(f32[768]{0:T(1024)} %get-tuple-element.143) | copy-start | bytes 9220
  406.8 48.3 %copy-start.55 = (f32[768]{0:T(1024)S(1)}, f32[768]{0:T(1024)}, u32[]{:S(2)}) copy-start(f32[768]{0:T(1024)} %get-tuple-element.144) | copy-start | bytes 9220
  406.8 48.9 %copy-start.54 = (f32[768]{0:T(1024)S(1)}, f32[768]{0:T(1024)}, u32[]{:S(2)}) copy-start(f32[768]{0:T(1024)} %get-tuple-element.145) | copy-start | bytes 9220
  406.8 49.5 %copy-start.64 = (f32[768]{0:T(1024)S(1)}, f32[768]{0:T(1024)}, u32[]{:S(2)}) copy-start(f32[768]{0:T(1024)} %get-tuple-element.128) | copy-start | bytes 9220
  406.8 50.1 %copy-start.53 = (f32[768]{0:T(1024)S(1)}, f32[768]{0:T(1024)}, u32[]{:S(2)}) copy-start(f32[768]{0:T(1024)} %get-tuple-element.155) | copy-start | bytes 9220
  406.8 50.7 %copy-start.52 = (f32[768]{0:T(1024)S(1)}, f32[768]{0:T(1024)}, u32[]{:S(2)}) copy-start(f32[768]{0:T(1024)} %get-tuple-element.156) | copy-start | bytes 9220
  406.8 51.2 %copy-start.51 = (f32[768]{0:T(1024)S(1)}, f32[768]{0:T(1024)}, u32[]{:S(2)}) copy-start(f32[768]{0:T(1024)} %get-tuple-element.157) | copy-start | bytes 9220
  406.9 51.8 %copy-start.50 = (f32[768]{0:T(1024)S(1)}, f32[768]{0:T(1024)}, u32[]{:S(2)}) copy-start(f32[768]{0:T(1024)} %get-tuple-element.158) | copy-start | bytes 9220
  406.9 52.4 %copy-start.49 = (f32[768]{0:T(1024)S(1)}, f32[768]{0:T(1024)}, u32[]{:S(2)}) copy-start(f32[768]{0:T(1024)} %get-tuple-element.159) | copy-start | bytes 9220
  406.9 53.0 %copy-start.48 = (f32[768]{0:T(1024)S(1)}, f32[768]{0:T(1024)}, u32[]{:S(2)}) copy-start(f32[768]{0:T(1024)} %get-tuple-element.160) | copy-start | bytes 9220
  406.9 53.6 %copy-start.47 = (f32[768]{0:T(1024)S(1)}, f32[768]{0:T(1024)}, u32[]{:S(2)}) copy-start(f32[768]{0:T(1024)} %get-tuple-element.161) | copy-start | bytes 9220
  406.9 54.1 %copy-start.46 = (f32[768]{0:T(1024)S(1)}, f32[768]{0:T(1024)}, u32[]{:S(2)}) copy-start(f32[768]{0:T(1024)} %get-tuple-element.162) | copy-start | bytes 9220
  406.9 54.7 %copy-start.44 = (f32[768]{0:T(1024)S(1)}, f32[768]{0:T(1024)}, u32[]{:S(2)}) copy-start(f32[768]{0:T(1024)} %get-tuple-element.163) | copy-start | bytes 9220
  406.9 55.3 %copy-start.45 = (f32[768]{0:T(1024)S(1)}, f32[768]{0:T(1024)}, u32[]{:S(2)}) copy-start(f32[768]{0:T(1024)} %get-tuple-element.129) | copy-start | bytes 9220
  406.9 55.9 %copy-start.43 = (f32[768]{0:T(1024)S(1)}, f32[768]{0:T(1024)}, u32[]{:S(2)}) copy-start(f32[768]{0:T(1024)} %get-tuple-element.130) | copy-start | bytes 9220
  406.9 56.5 %copy-start.42 = (f32[768]{0:T(1024)S(1)}, f32[768]{0:T(1024)}, u32[]{:S(2)}) copy-start(f32[768]{0:T(1024)} %get-tuple-element.131) | copy-start | bytes 9220
  406.9 57.0 %copy-start.41 = (f32[768]{0:T(1024)S(1)}, f32[768]{0:T(1024)}, u32[]{:S(2)}) copy-start(f32[768]{0:T(1024)} %get-tuple-element.132) | copy-start | bytes 9220
  407.0 57.6 %copy-start.40 = (f32[768]{0:T(1024)S(1)}, f32[768]{0:T(1024)}, u32[]{:S(2)}) copy-start(f32[768]{0:T(1024)} %get-tuple-element.133) | copy-start | bytes 9220
  407.0 58.2 %copy-start.39 = (f32[768]{0:T(1024)S(1)}, f32[768]{0:T(1024)}, u32[]{:S(2)}) copy-start(f32[768]{0:T(1024)} %get-tuple-element.134) | copy-start | bytes 9220
  407.0 58.8 %copy-start.38 = (f32[768]{0:T(1024)S(1)}, f32[768]{0:T(1024)}, u32[]{:S(2)}) copy-start(f32[768]{0:T(1024)} %get-tuple-element.135) | copy-start | bytes 9220
  407.0 59.4 %copy-start.37 = (f32[768]{0:T(1024)S(1)}, f32[768]{0:T(1024)}, u32[]{:S(2)}) copy-start(f32[768]{0:T(1024)} %get-tuple-element.136) | copy-start | bytes 9220
  407.0 60.1 %copy-start.16 = (f32[256,12]{0,1:T(8,128)S(1)}, f32[256,12]{0,1:T(8,128)}, u32[]{:S(2)}) copy-start(f32[256,12]{0,1:T(8,128)} %copy-done.15) | copy-start | bytes 36868
  407.0 60.1 %copy-start.4 = (bf16[12,256,256]{2,1,0:T(8,128)(2,1)S(1)}, bf16[12,256,256]{2,1,0:T(8,128)(2,1)}, u32[]{:S(2)}) copy-start(bf16[12,256,256]{2,1,0:T(8,128)(2,1)} %get-tuple-element.50) | copy-start | bytes 4718596
  468.4 26.5 %copy-start.5 = (bf16[256,768]{1,0:T(8,128)(2,1)S(1)}, bf16[256,768]{1,0:T(8,128)(2,1)}, u32[]{:S(2)}) copy-start(bf16[256,768]{1,0:T(8,128)(2,1)} %param.21) | copy-start | bytes 1179652
  496.9 33.9 %copy-start.31 = (f32[768]{0:T(1024)S(1)}, f32[768]{0:T(1024)}, u32[]{:S(2)}) copy-start(f32[768]{0:T(1024)} %get-tuple-element.193) | copy-start | bytes 9220
  496.9 33.9 %copy-start.32 = (f32[768]{0:T(1024)S(1)}, f32[768]{0:T(1024)}, u32[]{:S(2)}) copy-start(f32[768]{0:T(1024)} %get-tuple-element.196) | copy-start | bytes 9220
  496.9 33.9 %copy-start.33 = (f32[768]{0:T(1024)S(1)}, f32[768]{0:T(1024)}, u32[]{:S(2)}) copy-start(f32[768]{0:T(1024)} %get-tuple-element.286) | copy-start | bytes 9220
  496.9 33.9 %copy-start.34 = (f32[768]{0:T(1024)S(1)}, f32[768]{0:T(1024)}, u32[]{:S(2)}) copy-start(f32[768]{0:T(1024)} %get-tuple-element.126) | copy-start | bytes 9220
  496.9 33.9 %copy-start.35 = (f32[768]{0:T(1024)S(1)}, f32[768]{0:T(1024)}, u32[]{:S(2)}) copy-start(f32[768]{0:T(1024)} %get-tuple-element.195) | copy-start | bytes 9220
  496.9 33.9 %copy-start.36 = (f32[768]{0:T(1024)S(1)}, f32[768]{0:T(1024)}, u32[]{:S(2)}) copy-start(f32[768]{0:T(1024)} %get-tuple-element.288) | copy-start | bytes 9220
  496.9 99.2 %copy-start.3 = (f32[256,768]{1,0:T(8,128)S(1)}, f32[256,768]{1,0:T(8,128)}, u32[]{:S(2)}) copy-start(f32[256,768]{1,0:T(8,128)} %copy-done.2) | copy-start | bytes 2359300
  496.9 99.2 %copy-start.121 = (f32[256]{0:T(256)S(1)}, f32[256]{0:T(256)}, u32[]{:S(2)}) copy-start(f32[256]{0:T(256)} %copy-done.120) | copy-start | bytes 3076
  (70 other events, 431.6 us)
Sparse Core Ops, SparseCore 0:
  88.9 65.6 all-gather.1
  171.0 76.4 reduce-scatter.2
  301.4 79.4 reduce-scatter.4
  383.9 120.1 all-reduce.10
  510.0 157.3 all-reduce.8
